TPU v7x, 256 devices: a whole 4x4x8 slice. The times are simulated.
256 devices in a mesh: rec: 32 (over z, x), ani: 4 (over y_lo, core), chain: 2 (over y_hi).
Axes of the slice: x: 4, y: 4 (y_hi: 2, y_lo: 2; y = y_hi * 2 + y_lo), z: 8, core: 2. Of those that a mesh axis runs over, the one named last changes fastest.
Arguments:
- genotypes: bfloat16 [131072, 4096], P('ani', 'rec'), may hold values from -0.09375 to 0.09375
- effects: float32 [8192], P(('chain', 'rec')), parts along dimension 0, may hold values from -6 to 6
- gaussian_draw: float32 [8192], P(('chain', 'rec')), parts along dimension 0, may hold values from -6 to 6
- prior_prec: float32 [4096], P('rec'), may hold values from 2 to 40
- accept: int32 [64], P(('chain', 'rec')), parts along dimension 0, may hold values 0 or 1
- herd_effect: float32 [131072], P(('chain', 'rec')), parts along dimension 0, may hold values from -6 to 6
- phenotype: float32 [1048576], P(('rec', 'ani')), may hold values from -12 to 12
- record_animal: int32 [1048576], P(('rec', 'ani')), may hold values from 0 to 131071
- record_bin: int32 [1048576], P(('rec', 'ani')), may hold values from 0 to 65535, as said below
- live_records: int32 [128], P(('rec', 'ani')), may hold values from 1 to 8192, 655360 in all
Outputs:
- next_effects: float32 [8192], P(('chain', 'rec')), parts along dimension 0
- resid_sum: float32 [262144], P(('chain', 'ani')), parts along dimension 0
There are 2 independent parts, one for each index of `chain`. A program takes and returns all parts, laid end to end along the dimension named above; an argument that names none is the same for every part. Nothing has to cross between parts.
Inputs may be any that keep to these rules, and one draw needn't show every extreme that they name: `record_bin`: a record held by rec index k names a group of k * 2048 to (k + 1) * 2048 - 1.
All inputs are finite; a program needn't handle non-finite values. No bound on the sum of `accept` or of `live_records` on one device may be relied on, other than what follows from the above.
Results may differ from a plain program's by a relative error of at most 0.0033.
Values sent between devices are 32-bit elements; how exact they have to be, the bound alone decides.
A program may use at most 64 MiB of HBM per device.

v0:
```python
import math
import jax
import jax.numpy as jnp
from jax import lax
from jax.sharding import PartitionSpec as P

BLOCK = 128


def on_device(
    genotypes,
    effects,
    gaussian_draw,
    prior_prec,
    accept,
    herd_effect,
    phenotype,
    record_animal,
    record_bin,
    live_records,
):
    step_size = 0.005
    effects_half = effects.astype(jnp.bfloat16)
    partial_value = jnp.dot(genotypes, effects_half, preferred_element_type=jnp.float32)
    breeding_block = lax.psum(partial_value, "rec")
    breeding = lax.all_gather(breeding_block, "ani", axis=0, tiled=True)
    local_bin = record_bin - lax.axis_index("rec") * herd_effect.shape[0]
    position = jnp.arange(phenotype.shape[0], dtype=jnp.int32)
    live = position < live_records[0]
    herd_value = jnp.take(herd_effect, local_bin)
    residual = jnp.where(
        live, phenotype - herd_value - jnp.take(breeding, record_animal), jnp.zeros_like(phenotype)
    )
    animals = breeding.shape[0]
    partial_sums = jax.ops.segment_sum(residual, record_animal, num_segments=animals)
    share = lax.psum_scatter(partial_sums, "ani", scatter_dimension=0, tiled=True)
    resid_sum = lax.psum(share, "rec")
    resid_half = resid_sum.astype(jnp.bfloat16)
    grad_part = jnp.dot(resid_half, genotypes, preferred_element_type=jnp.float32)
    likelihood_grad = lax.psum(grad_part, "ani")
    gradient = likelihood_grad - prior_prec * effects
    proposal = effects + step_size * gradient + math.sqrt(2.0 * step_size) * gaussian_draw
    accepted = jnp.repeat(accept, BLOCK) == 1
    return (jnp.where(accepted, proposal, effects), resid_sum)


def solution(mesh):
    return jax.shard_map(
        on_device,
        mesh=mesh,
        in_specs=(
            P("ani", "rec"),
            P(("chain", "rec")),
            P(("chain", "rec")),
            P("rec"),
            P(("chain", "rec")),
            P(("chain", "rec")),
            P(("rec", "ani")),
            P(("rec", "ani")),
            P(("rec", "ani")),
            P(("rec", "ani")),
        ),
        out_specs=(P(("chain", "rec")), P(("chain", "ani"))),
        check_vma=False,
    )
```

profile of v0, /device:TPU:1, one launch (start us, length us, event | category | flops | bytes accessed | tf_op | source)
XLA Modules:
  0.0 464.9 jit_solution(7304369323534873181)
XLA Ops:
  7.2 0.0 copy-start
  7.2 0.0 copy-start.2
  7.2 0.0 all-reduce.5.cloned.1.call-start
  7.2 6.3 %fusion.4 = f32[1,32768]{1,0:T(1,128)} fusion(bf16[32768,128]{1,0:T(8,128)(2,1)} %param.10, f32[128]{0:T(128)} %param.11), kind=kOutput, calls=%fused_computation.13 | convolution fusion | flops 8388736 | bytes 8520192 | tf_op jit(solution)/shard_map/dot_general | solution.py:24
  13.5 0.0 all-reduce.5.cloned.1.call-update
  13.6 0.0 all-reduce.9.cloned.1.call-start
  14.3 0.0 copy-done.2
  14.3 0.0 copy-done
  14.3 0.0 copy-start.3
  14.3 45.5 %gather_fusion = f32[8192]{0:T(1024)S(1)} fusion(f32[2048]{0:T(1024)S(1)} %copy-done, s32[8192]{0:T(1024)S(1)} %fusion.3), kind=kCustom, calls=%fused_computation | custom fusion | bytes 98304 | tf_op jit(solution)/shard_map/jit(_take)/gather | solution.py:30
  59.9 0.0 copy-done.3
  59.9 95.9 %all-reduce.5.cloned.1.call-done = f32[32768]{0:T(1024)} async-done(((f32[32768]{0:T(1024)}), f32[32768]{0:T(1024)}) %all-reduce.5.cloned.1.call-update) | async-done | bytes 131088 | tf_op jit(solution)/shard_map/psum | solution.py:25
  155.8 12.2 %all_gather.3 = f32[131072]{0:T(1024)S(1)} all-gather(f32[32768]{0:T(1024)} %all-reduce.5.cloned.1.call-done), channel_id=1, replica_groups=mesh['rec'=32,'ani'=4,'chain'=2] {'ani'}, dimensions={0}, use_global_device_ids=true | all-gather | bytes 655360 | tf_op jit(solution)/shard_map/all_gather | solution.py:26
  167.9 0.0 copy-start.4
  167.9 0.0 copy-start.8
  167.9 45.5 %gather_fusion.1 = f32[8192]{0:T(1024)S(1)} fusion(f32[131072]{0:T(1024)S(1)} %all_gather.3, s32[8192]{0:T(1024)S(1)} %fusion.2), kind=kCustom, calls=%fused_computation.1 | custom fusion | bytes 98304 | tf_op jit(solution)/shard_map/jit(_take)/gather | solution.py:32
  213.5 0.0 copy-done.4
  213.5 44.0 %scatter_custom_fusion = f32[131072]{0:T(1024)} fusion(s32[8192]{0:T(1024)S(1)} %copy-done.3, f32[8192]{0:T(1024)S(1)} %subtract_select_fusion, f32[]{:T(128)} %constant.22.clone.1), kind=kCustom, calls=%fused_computation.4 | custom fusion | flops 8192 | bytes 524292 | tf_op jit(solution)/shard_map/scatter-add | solution.py:35
  257.5 0.0 all-reduce.9.cloned.1.call-update
  257.5 0.0 all-reduce.7.cloned.1.call-start
  257.6 0.0 copy-done.8
  257.6 0.6 dynamic-slice
  258.8 40.0 %all-reduce.9.cloned.1.call-done = f32[131072]{0:T(1024)} async-done(((f32[131072]{0:T(1024)}), f32[131072]{0:T(1024)}) %all-reduce.9.cloned.1.call-update) | async-done | bytes 524304
  298.8 1.6 dynamic-slice.1
  300.4 0.0 all-reduce.7.cloned.1.call-update
  301.0 140.5 %all-reduce.7.cloned.1.call-done = f32[32768]{0:T(1024)} async-done(((f32[32768]{0:T(1024)}), f32[32768]{0:T(1024)}) %all-reduce.7.cloned.1.call-update) | async-done | bytes 131088 | tf_op jit(solution)/shard_map/psum | solution.py:37
  441.6 0.9 convert_element_type.7
  442.5 0.1 reshape.47
  442.6 0.0 copy-start.5
  442.6 0.0 copy-start.6
  442.6 0.0 copy-start.7
  442.6 0.0 copy-start.1
  442.6 4.6 convolution_bitcast_fusion
  447.2 10.0 %psum.23 = f32[128]{0:T(128)S(1)} all-reduce(f32[128]{0:T(128)S(1)} %convolution_bitcast_fusion), channel_id=1, replica_groups=mesh['rec'=32,'ani'=4,'chain'=2] {'ani'}, use_global_device_ids=true, to_apply=%region_4.5 | all-reduce | flops 128 | bytes 1024 | tf_op jit(solution)/shard_map/psum | solution.py:40
  457.2 0.0 copy-done.5
  457.2 0.0 copy-done.6
  457.2 0.0 copy-done.7
  457.2 0.5 broadcast_select_fusion
  457.7 0.0 copy-done.1
  457.7 0.7 copy.17
  (3 shorter events, 0.1 us)
Async XLA Ops:
  7.2 7.1 %copy-start = (f32[2048]{0:T(1024)S(1)}, f32[2048]{0:T(1024)}, u32[]{:S(2)}) copy-start(f32[2048]{0:T(1024)} %param.15) | copy-start | bytes 24580
  7.2 7.1 %copy-start.2 = (s32[8192]{0:T(1024)S(1)}, s32[8192]{0:T(1024)}, u32[]{:S(2)}) copy-start(s32[8192]{0:T(1024)} %param.18) | copy-start | bytes 98308
  7.2 148.6 %all-reduce.5.cloned.1.call-start = ((), (), s32[]{:S(2)}) async-start(), calls=%async_computation | async-start | bytes 262144 | tf_op jit(solution)/shard_map/psum | solution.py:25
  13.6 285.2 %all-reduce.9.cloned.1.call-start = ((), (), s32[]{:S(2)}) async-start(), calls=%async_computation.2 | async-start | bytes 1048576
  14.3 45.6 %copy-start.3 = (s32[8192]{0:T(1024)S(1)}, s32[8192]{0:T(1024)}, u32[]{:S(2)}) copy-start(s32[8192]{0:T(1024)} %param.17) | copy-start | bytes 98308
  167.9 45.5 %copy-start.4 = (f32[8192]{0:T(1024)S(1)}, f32[8192]{0:T(1024)}, u32[]{:S(2)}) copy-start(f32[8192]{0:T(1024)} %param.16) | copy-start | bytes 98308
  167.9 89.6 %copy-start.8 = (u32[256]{0:T(256)S(1)}, u32[256]{0:T(256)}, u32[]{:S(2)}) copy-start(u32[256]{0:T(256)} %constant.51) | copy-start | bytes 3076
  257.5 184.1 %all-reduce.7.cloned.1.call-start = ((), (), s32[]{:S(2)}) async-start(), calls=%async_computation.1 | async-start | bytes 262144 | tf_op jit(solution)/shard_map/psum | solution.py:37
  442.6 14.6 %copy-start.5 = (f32[128]{0:T(128)S(1)}, f32[128]{0:T(128)}, u32[]{:S(2)}) copy-start(f32[128]{0:T(128)} %param.11) | copy-start | bytes 1540
  442.6 14.6 %copy-start.6 = (f32[128]{0:T(128)S(1)}, f32[128]{0:T(128)}, u32[]{:S(2)}) copy-start(f32[128]{0:T(128)} %param.12) | copy-start | bytes 1540
  442.6 14.6 %copy-start.7 = (f32[128]{0:T(128)S(1)}, f32[128]{0:T(128)}, u32[]{:S(2)}) copy-start(f32[128]{0:T(128)} %param.13) | copy-start | bytes 1540
  442.6 15.1 %copy-start.1 = (f32[32768]{0:T(1024)S(1)}, f32[32768]{0:T(1024)}, u32[]{:S(2)}) copy-start(f32[32768]{0:T(1024)} %all-reduce.7.cloned.1.call-done) | copy-start | bytes 393220
Sparse Core Ops, SparseCore 0:
  13.7 142.0 all-reduce.4
  257.6 41.1 all-reduce.8
  302.8 138.7 all-reduce.6
where the time goes:
time: 465 us
  waiting for transfers between devices  276 us (59%)
  local copies, waits for them, and re-layouts  94 us (20%)
  other arithmetic  45.5 us (10%)
  blocking collectives  22.1 us (5%)
  between operations  15.8 us (3%)
  matrix products  10.9 us (2%)
    psum x1, waiting for transfers between devices, on_device(): resid_sum = lax.psum(share, 'rec')  141 us
    psum x1, waiting for transfers between devices, on_device(): breeding_block = lax.psum(partial_value, 'rec')  95.9 us
    gather x1, local copies, waits for them, and re-layouts, on_device(): herd_value = jnp.take(herd_effect, local_bin)  45.5 us
    gather x1, local copies, waits for them, and re-layouts, on_device(): jnp.take(breeding, record_animal)  45.5 us
    scatter-add x1, other arithmetic, on_device(): jax.ops.segment_sum(residual, record_animal, num_segments=animals)  44 us
    unnamed x4, waiting for transfers between devices  40 us
    all_gather x1, blocking collectives, on_device(): breeding = lax.all_gather(breeding_block, 'ani', axis=0, tiled=True)  12.2 us
    psum x1, blocking collectives, on_device(): likelihood_grad = lax.psum(grad_part, 'ani')  9.98 us
  transfers between devices with their start and end apart: 3, of which 3 were waited for; matrix products, arithmetic and copies ran while one was open for 10% of the time, Pallas kernels for 0%

commit v1 on v0

--- a/solution.py
+++ b/solution.py
@@ -22,7 +22,8 @@
     step_size = 0.005
     effects_half = effects.astype(jnp.bfloat16)
     partial_value = jnp.dot(genotypes, effects_half, preferred_element_type=jnp.float32)
-    breeding_block = lax.psum(partial_value, "rec")
+    parts = lax.all_gather(partial_value, "rec")
+    breeding_block = jnp.sum(parts, axis=0)
     breeding = lax.all_gather(breeding_block, "ani", axis=0, tiled=True)
     local_bin = record_bin - lax.axis_index("rec") * herd_effect.shape[0]
     position = jnp.arange(phenotype.shape[0], dtype=jnp.int32)

time: 465 us -> 410 us (0.88)
  waiting for transfers between devices: 276 us -> 215 us
  local copies, waits for them, and re-layouts: 94 us -> 99 us
    psum x1 -> x0, waiting for transfers between devices: 95.9 us -> none  [on_device(): breeding_block = lax.psum(partial_value, 'rec')]
    all_gather x0 -> x1, waiting for transfers between devices: none -> 35.8 us  [on_device(): parts = lax.all_gather(partial_value, 'rec')]
    all_gather x0 -> x1, local copies, waits for them, and re-layouts: none -> 4.97 us  [on_device(): parts = lax.all_gather(partial_value, 'rec')]
  transfers between devices with their start and end apart: 3 -> 3, of which waited for: 3 -> 3; matrix products, arithmetic and copies ran while one was open for 10% -> 11% of each run, Pallas kernels for 0% -> 0%
where the time goes in v1:
time: 410 us
  waiting for transfers between devices  215 us (52%)
  local copies, waits for them, and re-layouts  99 us (24%)
  other arithmetic  48.1 us (12%)
  blocking collectives  21.2 us (5%)
  between operations  15.8 us (4%)
  matrix products  10.9 us (3%)
    psum x1, waiting for transfers between devices, on_device(): resid_sum = lax.psum(share, 'rec')  141 us
    gather x1, local copies, waits for them, and re-layouts, on_device(): herd_value = jnp.take(herd_effect, local_bin)  45.5 us
    gather x1, local copies, waits for them, and re-layouts, on_device(): jnp.take(breeding, record_animal)  45.5 us
    scatter-add x1, other arithmetic, on_device(): jax.ops.segment_sum(residual, record_animal, num_segments=animals)  44 us
    unnamed x4, waiting for transfers between devices  38.5 us
    all_gather x1, waiting for transfers between devices, on_device(): parts = lax.all_gather(partial_value, 'rec')  35.8 us
    all_gather x1, blocking collectives, on_device(): breeding = lax.all_gather(breeding_block, 'ani', axis=0, tiled=True)  11.2 us
    psum x1, blocking collectives, on_device(): likelihood_grad = lax.psum(grad_part, 'ani')  9.98 us
  transfers between devices with their start and end apart: 3, of which 3 were waited for; matrix products, arithmetic and copies ran while one was open for 11% of the time, Pallas kernels for 0%

profile of v1, /device:TPU:1, one launch (start us, length us, event | category | flops | bytes accessed | tf_op | source)
XLA Modules:
  0.0 410.0 jit_solution(11379704333208392283)
XLA Ops:
  7.2 0.0 copy-start
  7.2 0.0 copy-start.2
  7.2 0.0 all-gather.3.cloned.1.call-start
  7.2 6.3 %fusion.4 = f32[1,32768]{1,0:T(1,128)} fusion(bf16[32768,128]{1,0:T(8,128)(2,1)} %param.10, f32[128]{0:T(128)} %param.11), kind=kOutput, calls=%fused_computation.13 | convolution fusion | flops 8388736 | bytes 8520192 | tf_op jit(solution)/shard_map/dot_general | solution.py:24
  13.5 0.0 all-gather.3.cloned.1.call-update
  13.6 0.0 all-reduce.6.cloned.1.call-start
  14.3 0.0 copy-done.2
  14.3 0.0 copy-done
  14.3 0.0 copy-start.3
  14.3 45.5 %gather_fusion = f32[8192]{0:T(1024)S(1)} fusion(f32[2048]{0:T(1024)S(1)} %copy-done, s32[8192]{0:T(1024)S(1)} %fusion.3), kind=kCustom, calls=%fused_computation | custom fusion | bytes 98304 | tf_op jit(solution)/shard_map/jit(_take)/gather | solution.py:31
  59.9 0.0 copy-done.3
  59.9 35.8 %all-gather.3.cloned.1.call-done = f32[1048576]{0:T(1024)} async-done(((f32[32768]{0:T(1024)}), f32[1048576]{0:T(1024)}) %all-gather.3.cloned.1.call-update) | async-done | bytes 4194320 | tf_op jit(solution)/shard_map/all_gather | solution.py:25
  95.7 5.0 %reshape.42 = f32[32,32768]{1,0:T(8,128)} reshape(f32[1048576]{0:T(1024)} %all-gather.3.cloned.1.call-done) | data formatting | bytes 8388608 | tf_op jit(solution)/shard_map/all_gather | solution.py:25
  100.7 2.6 reduce_sum.9
  103.3 11.2 %all_gather.11 = f32[131072]{0:T(1024)S(1)} all-gather(f32[32768]{0:T(1024)S(1)} %reduce_sum.9), channel_id=1, replica_groups=mesh['rec'=32,'ani'=4,'chain'=2] {'ani'}, dimensions={0}, use_global_device_ids=true | all-gather | bytes 655360 | tf_op jit(solution)/shard_map/all_gather | solution.py:27
  114.5 0.0 copy-start.4
  114.5 0.0 copy-start.8
  114.5 45.5 %gather_fusion.1 = f32[8192]{0:T(1024)S(1)} fusion(f32[131072]{0:T(1024)S(1)} %all_gather.11, s32[8192]{0:T(1024)S(1)} %fusion.2), kind=kCustom, calls=%fused_computation.1 | custom fusion | bytes 98304 | tf_op jit(solution)/shard_map/jit(_take)/gather | solution.py:33
  160.1 0.0 copy-done.4
  160.1 44.0 %scatter_custom_fusion = f32[131072]{0:T(1024)} fusion(s32[8192]{0:T(1024)S(1)} %copy-done.3, f32[8192]{0:T(1024)S(1)} %subtract_select_fusion, f32[]{:T(128)} %constant.22.clone.1), kind=kCustom, calls=%fused_computation.4 | custom fusion | flops 8192 | bytes 524292 | tf_op jit(solution)/shard_map/scatter-add | solution.py:36
  204.1 0.0 all-reduce.6.cloned.1.call-update
  204.1 0.0 all-reduce.4.cloned.1.call-start
  204.2 0.0 copy-done.8
  204.2 0.6 dynamic-slice
  205.4 38.5 %all-reduce.6.cloned.1.call-done = f32[131072]{0:T(1024)} async-done(((f32[131072]{0:T(1024)}), f32[131072]{0:T(1024)}) %all-reduce.6.cloned.1.call-update) | async-done | bytes 524304
  243.9 1.6 dynamic-slice.1
  245.4 0.0 all-reduce.4.cloned.1.call-update
  246.1 140.5 %all-reduce.4.cloned.1.call-done = f32[32768]{0:T(1024)} async-done(((f32[32768]{0:T(1024)}), f32[32768]{0:T(1024)}) %all-reduce.4.cloned.1.call-update) | async-done | bytes 131088 | tf_op jit(solution)/shard_map/psum | solution.py:38
  386.7 0.9 convert_element_type.7
  387.6 0.1 reshape.48
  387.6 0.0 copy-start.5
  387.6 0.0 copy-start.6
  387.7 0.0 copy-start.7
  387.7 0.0 copy-start.1
  387.7 4.6 %convolution_bitcast_fusion = f32[128]{0:T(128)S(1)} fusion(bf16[32768,1]{0,1:T(2,128)(2,1)S(1)} %reshape.48, bf16[32768,128]{1,0:T(8,128)(2,1)} %param.10), kind=kOutput, calls=%fused_computation.3 | convolution fusion | flops 8388608 | bytes 8454656 | tf_op jit(solution)/shard_map/dot_general | solution.py:40
  392.3 10.0 %psum.15 = f32[128]{0:T(128)S(1)} all-reduce(f32[128]{0:T(128)S(1)} %convolution_bitcast_fusion), channel_id=1, replica_groups=mesh['rec'=32,'ani'=4,'chain'=2] {'ani'}, use_global_device_ids=true, to_apply=%region_4.5 | all-reduce | flops 128 | bytes 1024 | tf_op jit(solution)/shard_map/psum | solution.py:41
  402.3 0.0 copy-done.5
  402.3 0.0 copy-done.6
  402.3 0.0 copy-done.7
  402.3 0.5 broadcast_select_fusion
  402.8 0.0 copy-done.1
  402.8 0.7 copy.16
  (3 shorter events, 0.1 us)
Async XLA Ops:
  7.2 7.1 %copy-start = (f32[2048]{0:T(1024)S(1)}, f32[2048]{0:T(1024)}, u32[]{:S(2)}) copy-start(f32[2048]{0:T(1024)} %param.15) | copy-start | bytes 24580
  7.2 7.1 %copy-start.2 = (s32[8192]{0:T(1024)S(1)}, s32[8192]{0:T(1024)}, u32[]{:S(2)}) copy-start(s32[8192]{0:T(1024)} %param.18) | copy-start | bytes 98308
  7.2 88.5 %all-gather.3.cloned.1.call-start = ((), (), s32[]{:S(2)}) async-start(), calls=%async_computation.1 | async-start | bytes 4325376 | tf_op jit(solution)/shard_map/all_gather | solution.py:25
  13.6 230.3 %all-reduce.6.cloned.1.call-start = ((), (), s32[]{:S(2)}) async-start(), calls=%async_computation.2 | async-start | bytes 1048576
  14.3 45.6 %copy-start.3 = (s32[8192]{0:T(1024)S(1)}, s32[8192]{0:T(1024)}, u32[]{:S(2)}) copy-start(s32[8192]{0:T(1024)} %param.17) | copy-start | bytes 98308
  114.5 45.5 %copy-start.4 = (f32[8192]{0:T(1024)S(1)}, f32[8192]{0:T(1024)}, u32[]{:S(2)}) copy-start(f32[8192]{0:T(1024)} %param.16) | copy-start | bytes 98308
  114.5 89.6 %copy-start.8 = (u32[256]{0:T(256)S(1)}, u32[256]{0:T(256)}, u32[]{:S(2)}) copy-start(u32[256]{0:T(256)} %constant.52) | copy-start | bytes 3076
  204.1 182.5 %all-reduce.4.cloned.1.call-start = ((), (), s32[]{:S(2)}) async-start(), calls=%async_computation | async-start | bytes 262144 | tf_op jit(solution)/shard_map/psum | solution.py:38
  387.6 14.6 %copy-start.5 = (f32[128]{0:T(128)S(1)}, f32[128]{0:T(128)}, u32[]{:S(2)}) copy-start(f32[128]{0:T(128)} %param.11) | copy-start | bytes 1540
  387.6 14.6 %copy-start.6 = (f32[128]{0:T(128)S(1)}, f32[128]{0:T(128)}, u32[]{:S(2)}) copy-start(f32[128]{0:T(128)} %param.12) | copy-start | bytes 1540
  387.7 14.6 %copy-start.7 = (f32[128]{0:T(128)S(1)}, f32[128]{0:T(128)}, u32[]{:S(2)}) copy-start(f32[128]{0:T(128)} %param.13) | copy-start | bytes 1540
  387.7 15.1 %copy-start.1 = (f32[32768]{0:T(1024)S(1)}, f32[32768]{0:T(1024)}, u32[]{:S(2)}) copy-start(f32[32768]{0:T(1024)} %all-reduce.4.cloned.1.call-done) | copy-start | bytes 393220
Sparse Core Ops, SparseCore 0:
  13.7 81.9 all-gather.2
  204.2 39.5 all-reduce.5
  247.9 138.7 all-reduce.3
